TPU v7x, 32 devices: a whole 2x2x4 slice. The times are simulated.
32 devices in a mesh: group: 8 (over y, x, core), replica: 4 (over z).
Axes of the slice: x: 2, y: 2, z: 4, core: 2. Of those that a mesh axis runs over, the one named last changes fastest.
Arguments:
- inputs: bfloat16 [64, 512, 768], P(('group', 'replica')), may hold values from -6 to 6
- cotangent: bfloat16 [64, 512, 768], P(('group', 'replica')), may hold values from -6 to 6
- lengths: int32 [64], P(('group', 'replica')), may hold values from 128 to 512, as said below
- query_weight: bfloat16 [768, 768], P('group'), may hold values from -0.21875 to 0.21875
- key_weight: bfloat16 [768, 768], P('group'), may hold values from -0.21875 to 0.21875
- value_weight: bfloat16 [768, 768], P('group'), may hold values from -0.21875 to 0.21875
- out_weight: bfloat16 [768, 768], P('group'), may hold values from -3.5 to 3.5
- in_weight: bfloat16 [768, 3072], P('group'), may hold values from -0.21875 to 0.21875
- back_weight: bfloat16 [3072, 768], P('group'), may hold values from -0.109375 to 0.109375
- query_bias: bfloat16 [768], P('group'), may hold values from -1.796875 to 1.796875
- value_bias: bfloat16 [768], P('group'), may hold values from -1.796875 to 1.796875
- out_bias: bfloat16 [768], P('group'), may hold values from -1.796875 to 1.796875
- in_bias: bfloat16 [3072], P('group'), may hold values from -1.796875 to 1.796875
- back_bias: bfloat16 [768], P('group'), may hold values from -1.796875 to 1.796875
- first_gain: bfloat16 [768], P('group'), may hold values from 0.5 to 1.5
- first_shift: bfloat16 [768], P('group'), may hold values from -1.796875 to 1.796875
- second_gain: bfloat16 [768], P('group'), may hold values from 0.5 to 1.5
- second_shift: bfloat16 [768], P('group'), may hold values from -1.796875 to 1.796875
Outputs:
- layer_out: bfloat16 [64, 512, 768], P(('group', 'replica'))
- input_grad: bfloat16 [64, 512, 768], P(('group', 'replica'))
- query_weight_grad: float32 [768, 768], P('group')
- key_weight_grad: float32 [768, 768], P('group')
- value_weight_grad: float32 [768, 768], P('group')
- out_weight_grad: float32 [768, 768], P('group')
- in_weight_grad: float32 [768, 3072], P('group')
- back_weight_grad: float32 [3072, 768], P('group')
- query_bias_grad: float32 [768], P('group')
- value_bias_grad: float32 [768], P('group')
- out_bias_grad: float32 [768], P('group')
- in_bias_grad: float32 [3072], P('group')
- back_bias_grad: float32 [768], P('group')
- first_gain_grad: float32 [768], P('group')
- first_shift_grad: float32 [768], P('group')
- second_gain_grad: float32 [768], P('group')
- second_shift_grad: float32 [768], P('group')
Inputs may be any that keep to these rules, and one draw needn't show every extreme that they name: `lengths`: each sequence's valid tokens fill its first slots; some sequence has all 512 slots valid.
All inputs are finite; a program needn't handle non-finite values.
Results may differ from a plain program's by a relative error of at most 0.02.
Values may be sent and summed in bfloat16 or wider, within the bound.
No kernel may reach another device: no remote copies, remote signals or barrier semaphores. Data moves between devices by JAX's collectives and lax.ppermute only.
A program may use at most 192 MiB of HBM per device.

v0:
```python
import math
import jax
import jax.numpy as jnp
from jax import lax
from jax.sharding import PartitionSpec as P

HEADS = 12
HEAD_DIM = 64
NORM_EPS = 1e-12
inverse_root_two = 0.7071067811865476
inverse_root_tau = 0.3989422804014327


def for_sending(array):
    return jax.tree.map(lambda a: a.astype(jnp.bfloat16) if a.dtype == jnp.float32 else a, array)


def project(left, right):
    return jnp.dot(left, right, preferred_element_type=jnp.float32)


def outer_sum(left, right):
    return jnp.einsum("rd,re->de", left, right, preferred_element_type=jnp.float32)


def back_project(grad_rows, weight_full):
    return jnp.einsum("re,de->rd", grad_rows, weight_full, preferred_element_type=jnp.float32)


def norm_forward(hidden, norm_gain, norm_shift):
    centre = hidden - jnp.mean(hidden, -1, keepdims=True)
    inverse = lax.rsqrt(jnp.mean(centre * centre, -1, keepdims=True) + NORM_EPS)
    normed = centre * inverse
    return (normed * norm_gain + norm_shift, normed, inverse)


def norm_backward(grad_out, norm_gain, normed, inverse):
    scaled = grad_out * norm_gain
    centred = (
        scaled
        - jnp.mean(scaled, -1, keepdims=True)
        - normed * jnp.mean(scaled * normed, -1, keepdims=True)
    )
    return (inverse * centred, jnp.sum(grad_out * normed, 0), jnp.sum(grad_out, 0))


def gelu_slope(hidden):
    normal_cdf = 0.5 * (1.0 + lax.erf(hidden * inverse_root_two))
    density = jnp.exp(-0.5 * hidden * hidden) * inverse_root_tau
    return normal_cdf + hidden * density


def per_device(
    inputs,
    cotangent,
    lengths,
    query_weight,
    key_weight,
    value_weight,
    out_weight,
    in_weight,
    back_weight,
    query_bias,
    value_bias,
    out_bias,
    in_bias,
    back_bias,
    first_gain,
    first_shift,
    second_gain,
    second_shift,
):
    whole = (
        lax.all_gather(query_weight, "group", axis=0, tiled=True),
        lax.all_gather(key_weight, "group", axis=0, tiled=True),
        lax.all_gather(value_weight, "group", axis=0, tiled=True),
        lax.all_gather(out_weight, "group", axis=0, tiled=True),
        lax.all_gather(in_weight, "group", axis=0, tiled=True),
        lax.all_gather(back_weight, "group", axis=0, tiled=True),
        lax.all_gather(query_bias, "group", axis=0, tiled=True),
        lax.all_gather(value_bias, "group", axis=0, tiled=True),
        lax.all_gather(out_bias, "group", axis=0, tiled=True),
        lax.all_gather(in_bias, "group", axis=0, tiled=True),
        lax.all_gather(back_bias, "group", axis=0, tiled=True),
        lax.all_gather(first_gain, "group", axis=0, tiled=True),
        lax.all_gather(first_shift, "group", axis=0, tiled=True),
        lax.all_gather(second_gain, "group", axis=0, tiled=True),
        lax.all_gather(second_shift, "group", axis=0, tiled=True),
    )
    (
        full_query,
        full_key,
        full_value,
        full_out,
        full_in,
        full_back,
        bias_query,
        bias_value,
        bias_out,
        bias_in,
        bias_back,
        gain_first,
        shift_first,
        gain_second,
        shift_second,
    ) = whole
    seq_count, slot_count, model_width = inputs.shape
    total_rows = seq_count * slot_count
    block_rows = min(512, slot_count)
    seq_blocks = slot_count // block_rows
    item_count = seq_count * seq_blocks
    score_scale = 1.0 / math.sqrt(HEAD_DIM)
    flat_rows = inputs.reshape(total_rows, model_width)
    positions = lax.broadcasted_iota(jnp.int32, (seq_count, slot_count), 1)
    key_valid = positions < lengths[:, None]
    row_valid = key_valid.reshape(total_rows, 1).astype(jnp.float32)
    queries = (project(flat_rows, full_query) + bias_query.astype(jnp.float32)).astype(jnp.bfloat16)
    key_rows = project(flat_rows, full_key).astype(jnp.bfloat16)
    value_rows = (project(flat_rows, full_value) + bias_value.astype(jnp.float32)).astype(
        jnp.bfloat16
    )
    query_blocks = queries.reshape(item_count, block_rows, HEADS, HEAD_DIM)
    key_seqs = key_rows.reshape(seq_count, slot_count, HEADS, HEAD_DIM)
    value_seqs = value_rows.reshape(seq_count, slot_count, HEADS, HEAD_DIM)
    item_ids = jnp.arange(item_count, dtype=jnp.int32)

    def select_seq(item_id):
        seq_id = item_id // seq_blocks
        return (
            lax.dynamic_index_in_dim(key_seqs, seq_id, 0, False),
            lax.dynamic_index_in_dim(value_seqs, seq_id, 0, False),
            lax.dynamic_index_in_dim(key_valid, seq_id, 0, False),
        )

    def block_scores(query_part, key_part, valid_part):
        scores = (
            jnp.einsum("qhd,khd->hqk", query_part, key_part, preferred_element_type=jnp.float32)
            * score_scale
        )
        return jnp.where(valid_part[None, None, :], scores, -1e30)

    def attend(packed):
        query_part, item_id = packed
        key_part, value_part, valid_part = select_seq(item_id)
        scores = block_scores(query_part, key_part, valid_part)
        row_peak = jnp.max(scores, -1, keepdims=True)
        lifted = jnp.exp(scores - row_peak)
        normalizer = jnp.sum(lifted, -1, keepdims=True)
        soft_weights = (lifted / normalizer).astype(jnp.bfloat16)
        mixed_heads = jnp.einsum(
            "hqk,khd->qhd", soft_weights, value_part, preferred_element_type=jnp.float32
        )
        return (mixed_heads.astype(jnp.bfloat16), (row_peak + jnp.log(normalizer))[:, :, 0])

    mixed_blocks, log_sums = lax.map(attend, (query_blocks, item_ids))
    mixed_rows = mixed_blocks.reshape(total_rows, model_width)
    branch = project(mixed_rows, full_out) + bias_out.astype(jnp.float32)
    after_attn, normed_first, inverse_first = norm_forward(
        flat_rows.astype(jnp.float32) + branch,
        gain_first.astype(jnp.float32),
        shift_first.astype(jnp.float32),
    )
    after_low = after_attn.astype(jnp.bfloat16)
    hidden = project(after_low, full_in) + bias_in.astype(jnp.float32)
    active = jax.nn.gelu(hidden, approximate=False).astype(jnp.bfloat16)
    ffn_out = project(active, full_back) + bias_back.astype(jnp.float32)
    result_rows, normed_second, inverse_second = norm_forward(
        after_attn + ffn_out, gain_second.astype(jnp.float32), shift_second.astype(jnp.float32)
    )
    layer_out = result_rows.astype(jnp.bfloat16).reshape(seq_count, slot_count, model_width)
    again = (
        lax.all_gather(query_weight, "group", axis=0, tiled=True),
        lax.all_gather(key_weight, "group", axis=0, tiled=True),
        lax.all_gather(value_weight, "group", axis=0, tiled=True),
        lax.all_gather(out_weight, "group", axis=0, tiled=True),
        lax.all_gather(in_weight, "group", axis=0, tiled=True),
        lax.all_gather(back_weight, "group", axis=0, tiled=True),
        lax.all_gather(query_bias, "group", axis=0, tiled=True),
        lax.all_gather(value_bias, "group", axis=0, tiled=True),
        lax.all_gather(out_bias, "group", axis=0, tiled=True),
        lax.all_gather(in_bias, "group", axis=0, tiled=True),
        lax.all_gather(back_bias, "group", axis=0, tiled=True),
        lax.all_gather(first_gain, "group", axis=0, tiled=True),
        lax.all_gather(first_shift, "group", axis=0, tiled=True),
        lax.all_gather(second_gain, "group", axis=0, tiled=True),
        lax.all_gather(second_shift, "group", axis=0, tiled=True),
    )
    (
        back_query,
        back_key,
        back_value,
        back_out,
        back_in,
        back_ffn,
        unused_one,
        unused_two,
        unused_three,
        unused_four,
        unused_five,
        gain_first_b,
        unused_six,
        gain_second_b,
        unused_seven,
    ) = again
    grad_result = cotangent.reshape(total_rows, model_width).astype(jnp.float32) * row_valid
    grad_h2, second_gain_grad, second_shift_grad = norm_backward(
        grad_result, gain_second_b.astype(jnp.float32), normed_second, inverse_second
    )
    grad_ffn = grad_h2.astype(jnp.bfloat16)
    back_bias_grad = jnp.sum(grad_ffn.astype(jnp.float32), 0)
    back_weight_grad = outer_sum(active, grad_ffn)
    grad_hidden = (back_project(grad_ffn, back_ffn) * gelu_slope(hidden)).astype(jnp.bfloat16)
    in_bias_grad = jnp.sum(grad_hidden.astype(jnp.float32), 0)
    in_weight_grad = outer_sum(after_low, grad_hidden)
    grad_after = back_project(grad_hidden, back_in) + grad_h2
    grad_h1, first_gain_grad, first_shift_grad = norm_backward(
        grad_after, gain_first_b.astype(jnp.float32), normed_first, inverse_first
    )
    grad_branch = grad_h1.astype(jnp.bfloat16)
    out_bias_grad = jnp.sum(grad_branch.astype(jnp.float32), 0)
    out_weight_grad = outer_sum(mixed_rows, grad_branch)
    grad_mixed = back_project(grad_branch, back_out).astype(jnp.bfloat16)

    def attend_back(packed):
        query_part, grad_part, lse_part, item_id = packed
        key_part, value_part, valid_part = select_seq(item_id)
        scores = block_scores(query_part, key_part, valid_part)
        soft_weights = jnp.exp(scores - lse_part[:, :, None])
        grad_weights = jnp.einsum(
            "qhd,khd->hqk", grad_part, value_part, preferred_element_type=jnp.float32
        )
        grad_values = jnp.einsum(
            "hqk,qhd->khd",
            soft_weights.astype(jnp.bfloat16),
            grad_part,
            preferred_element_type=jnp.float32,
        )
        row_inner = jnp.sum(soft_weights * grad_weights, -1, keepdims=True)
        grad_scores = (soft_weights * (grad_weights - row_inner)).astype(jnp.bfloat16)
        grad_queries = (
            jnp.einsum("hqk,khd->qhd", grad_scores, key_part, preferred_element_type=jnp.float32)
            * score_scale
        )
        grad_keys = (
            jnp.einsum("hqk,qhd->khd", grad_scores, query_part, preferred_element_type=jnp.float32)
            * score_scale
        )
        return (grad_queries, grad_keys, grad_values)

    query_grad_blocks, key_grad_items, value_grad_items = lax.map(
        attend_back,
        (
            query_blocks,
            grad_mixed.reshape(item_count, block_rows, HEADS, HEAD_DIM),
            log_sums,
            item_ids,
        ),
    )
    grad_queries = query_grad_blocks.reshape(total_rows, model_width).astype(jnp.bfloat16)
    grad_keys = key_grad_items.reshape(seq_count, seq_blocks, slot_count, model_width).sum(1)
    grad_keys = grad_keys.reshape(total_rows, model_width).astype(jnp.bfloat16)
    grad_values = value_grad_items.reshape(seq_count, seq_blocks, slot_count, model_width).sum(1)
    grad_values = grad_values.reshape(total_rows, model_width).astype(jnp.bfloat16)
    query_bias_grad = jnp.sum(grad_queries.astype(jnp.float32), 0)
    value_bias_grad = jnp.sum(grad_values.astype(jnp.float32), 0)
    query_weight_grad = outer_sum(flat_rows, grad_queries)
    key_weight_grad = outer_sum(flat_rows, grad_keys)
    value_weight_grad = outer_sum(flat_rows, grad_values)
    input_rows = (
        grad_h1
        + back_project(grad_queries, back_query)
        + back_project(grad_keys, back_key)
        + back_project(grad_values, back_value)
    )
    input_grad = input_rows.astype(jnp.bfloat16).reshape(seq_count, slot_count, model_width)
    owned = (
        lax.psum_scatter(
            query_weight_grad.astype(jnp.bfloat16), "group", scatter_dimension=0, tiled=True
        ).astype(jnp.float32),
        lax.psum_scatter(
            key_weight_grad.astype(jnp.bfloat16), "group", scatter_dimension=0, tiled=True
        ).astype(jnp.float32),
        lax.psum_scatter(
            value_weight_grad.astype(jnp.bfloat16), "group", scatter_dimension=0, tiled=True
        ).astype(jnp.float32),
        lax.psum_scatter(
            out_weight_grad.astype(jnp.bfloat16), "group", scatter_dimension=0, tiled=True
        ).astype(jnp.float32),
        lax.psum_scatter(
            in_weight_grad.astype(jnp.bfloat16), "group", scatter_dimension=0, tiled=True
        ).astype(jnp.float32),
        lax.psum_scatter(
            back_weight_grad.astype(jnp.bfloat16), "group", scatter_dimension=0, tiled=True
        ).astype(jnp.float32),
        lax.psum_scatter(
            query_bias_grad.astype(jnp.bfloat16), "group", scatter_dimension=0, tiled=True
        ).astype(jnp.float32),
        lax.psum_scatter(
            value_bias_grad.astype(jnp.bfloat16), "group", scatter_dimension=0, tiled=True
        ).astype(jnp.float32),
        lax.psum_scatter(
            out_bias_grad.astype(jnp.bfloat16), "group", scatter_dimension=0, tiled=True
        ).astype(jnp.float32),
        lax.psum_scatter(
            in_bias_grad.astype(jnp.bfloat16), "group", scatter_dimension=0, tiled=True
        ).astype(jnp.float32),
        lax.psum_scatter(
            back_bias_grad.astype(jnp.bfloat16), "group", scatter_dimension=0, tiled=True
        ).astype(jnp.float32),
        lax.psum_scatter(
            first_gain_grad.astype(jnp.bfloat16), "group", scatter_dimension=0, tiled=True
        ).astype(jnp.float32),
        lax.psum_scatter(
            first_shift_grad.astype(jnp.bfloat16), "group", scatter_dimension=0, tiled=True
        ).astype(jnp.float32),
        lax.psum_scatter(
            second_gain_grad.astype(jnp.bfloat16), "group", scatter_dimension=0, tiled=True
        ).astype(jnp.float32),
        lax.psum_scatter(
            second_shift_grad.astype(jnp.bfloat16), "group", scatter_dimension=0, tiled=True
        ).astype(jnp.float32),
    )
    summed = tuple(
        jax.tree.map(
            lambda part: part.astype(jnp.float32), lax.psum(for_sending(tuple(owned)), "replica")
        )
    )
    return (layer_out, input_grad) + summed


def solution(mesh):
    return jax.shard_map(
        per_device,
        mesh=mesh,
        in_specs=(
            P(("group", "replica"), None, None),
            P(("group", "replica"), None, None),
            P(("group", "replica")),
            P("group", None),
            P("group", None),
            P("group", None),
            P("group", None),
            P("group", None),
            P("group", None),
            P("group"),
            P("group"),
            P("group"),
            P("group"),
            P("group"),
            P("group"),
            P("group"),
            P("group"),
            P("group"),
        ),
        out_specs=(
            P(("group", "replica"), None, None),
            P(("group", "replica"), None, None),
            P("group", None),
            P("group", None),
            P("group", None),
            P("group", None),
            P("group", None),
            P("group", None),
            P("group"),
            P("group"),
            P("group"),
            P("group"),
            P("group"),
            P("group"),
            P("group"),
            P("group"),
            P("group"),
        ),
        check_vma=False,
    )
```

profile of v0, /device:TPU:0, one launch (start us, length us, event | category | flops | bytes accessed | tf_op | source)
XLA Modules:
  0.0 681.8 jit_solution(8906284838521225156)
XLA Ops:
  19.8 25.9 %all-reduce.18 = (bf16[768]{0:T(1024)(128)(2,1)S(1)}, bf16[768]{0:T(1024)(128)(2,1)S(1)}, bf16[768]{0:T(1024)(128)(2,1)S(1)}, bf16[768]{0:T(1024)(128)(2,1)S(1)}...) all-reduce(bf16[768]{0:T(1024)(128)(2,1)S(1)} %dynamic-update-slice, ...), channel_id=1, replica_groups=mesh['group'=8,'replica'=4] {'group'}, use_global_device_ids=true, to_apply=%add.1 | all-reduce | flops 5376 | bytes 21504
  51.0 7.9 %all-gather = bf16[8,1,384]{2,1,0:T(2,128)(2,1)S(1)} all-gather(bf16[1,1,384]{2,1,0:T(2,128)(2,1)S(1)} %reshape.248), channel_id=1, replica_groups=mesh['group'=8,'replica'=4] {'group'}, dimensions={0}, use_global_device_ids=true | all-gather | bytes 6912 | tf_op jit(solution)/shard_map/all_gather | solution.py:83
  70.7 17.6 %all-gather.12.cloned.1.call-done = bf16[768,768]{1,0:T(8,128)(2,1)} async-done(((bf16[96,768]{1,0:T(8,128)(2,1)}), bf16[768,768]{1,0:T(8,128)(2,1)}) %all-gather.12.cloned.1.call-update) | async-done | bytes 1179664 | tf_op jit(solution)/shard_map/all_gather | solution.py:75
  88.4 4.3 convolution_convert_fusion.3
  98.6 25.4 %while.30 = (s32[]{:T(128)}, bf16[2,512,12,64]{1,3,2,0:T(8,128)(2,1)}, f32[2,12,512]{2,1,0:T(8,128)S(1)}, s32[2]{0:T(128)S(1)}, bf16[2,512,12,64]{1,3,2,0:T(8,12...) while((s32[]{:T(128)}, ...), condition=%wide.region_3.4_spmd, body=%wide.region_0.3_spmd.sunk | while | flops 843442176 | bytes 47426260 | solution.py:155
  134.7 19.9 %all-gather.16.cloned.1.call-done = bf16[768,3072]{1,0:T(8,128)(2,1)} async-done(((bf16[96,3072]{1,0:T(8,128)(2,1)}), bf16[768,3072]{1,0:T(8,128)(2,1)}) %all-gather.16.cloned.1.call-update) | async-done | bytes 4718608 | tf_op jit(solution)/shard_map/all_gather | solution.py:78
  154.6 37.4 %fusion.48 = (bf16[1024,3072]{1,0:T(8,128)(2,1)}, f32[1024,3072]{1,0:T(8,128)}) fusion(f32[3072]{0:T(1024)S(1)} %bitcast.208, bf16[768,3072]{1,0:T(8,128)(2,1)} %all-gather.16.cloned.1.call-done, f32[1024,768]{1,0:T(8,128)} %copy-done.6, f32[768]{0:T(1024)S(1)} %convert_element_type.280, f32[768]{0:T(1024)S(1)} %convert_element_type.279, ...), kind=kOutput, calls=%fused_computation.60 | convolution fusion | flops 5043388416 | bytes 26765312 | tf_op jit(solution)/shard_map/dot_general | solution.py:19
  195.2 9.3 %fusion.78 = (f32[1024]{0:T(1024)S(1)}, f32[1024,768]{1,0:T(8,128)S(1)}) fusion(f32[768]{0:T(1024)S(1)} %copy-done.51, bf16[1024,3072]{1,0:T(8,128)(2,1)} %get-tuple-element.468, bf16[3072,768]{1,0:T(8,128)(2,1)} %all-gather.18.cloned.1.call-done, f32[768]{0:T(1024)S(1)} %convert_element_type.280, f32[768]{0:T(1024)S(1)} %convert_element_type.279, ...), kind=kOutput, calls=%fused_computation.138 | convolution fusion | flops 4837342208 | bytes 17323008 | tf_op jit(solution)/shard_map/dot_general | solution.py:19
  211.3 13.4 %fusion.79 = (bf16[3072]{0:T(1024)(128)(2,1)}, bf16[1024,3072]{1,0:T(8,128)(2,1)S(1)}) fusion(f32[1024,3072]{1,0:T(8,128)} %get-tuple-element.469, f32[3072]{0:T(1024)S(1)} %bitcast.209, bf16[3072,768]{1,0:T(8,128)(2,1)S(1)} %copy-done.54, f32[1024,768]{1,0:T(8,128)S(1)} %get-tuple-element.454), kind=kOutput, calls=%fused_computation.139 | convolution fusion | flops 4870370304 | bytes 26757120 | tf_op jit(solution)/shard_map/re,de->rd/dot_general | solution.py:27
  224.8 6.6 multiply_reduce_fusion.2
  246.9 53.8 %while.31 = (s32[]{:T(128)}, bf16[2,512,12,64]{1,3,2,0:T(8,128)(2,1)}, bf16[2,512,12,64]{1,3,2,0:T(8,128)(2,1)}, bf16[2,512,12,64]{1,3,2,0:T(8,128)(2,1)}, s32[2...) while((s32[]{:T(128)}, ...), condition=%wide.region_14.15_spmd, body=%wide.region_12.14_spmd.sunk | while | flops 2061232128 | bytes 155120608 | solution.py:250
  254.9 7.3 %multiply_reduce_fusion.10 = (f32[12,512]{1,0:T(8,128)S(1)}, f32[12,512,512]{1,2,0:T(8,128)}) fusion(f32[12,512,512]{1,2,0:T(8,128)S(1)} %fusion.139, f32[12,512]{1,0:T(8,128)S(1)} %dynamic-slice_bitcast_fusion.2, pred[512]{0:T(512)(128)(4,1)S(1)} %dynamic-slice_reduce_fusion.5, bf16[2,512,12,64]{1,3,2,0:T(8,128)(2,1)S(1)} %copy-done.3, ...), kind=kOutput, calls=%fused_computation.23.clone.1 | convolution fusion | flops 418375680 | bytes 26796552 | tf_op jit(solution)/shard_map/while/body/eval_jaxpr/qhd,khd->hqk/dot_general | solution.py:229
  262.2 7.2 %multiply_convert_fusion.2 = bf16[12,512,512]{1,2,0:T(8,128)(2,1)S(1)} fusion(f32[12,512,512]{1,2,0:T(8,128)} %get-tuple-element.599, f32[12,512,512]{1,2,0:T(8,128)S(1)} %fusion.139, f32[12,512]{1,0:T(8,128)S(1)} %get-tuple-element.600, f32[12,512]{1,0:T(8,128)S(1)} %dynamic-slice_bitcast_fusion.2, pred[512]{0:T(512)(128)(4,1)S(1)} %dynamic-slice_reduce_fusion.5), kind=kLoop, calls=%fused_computation.22.clone.1 | loop fusion | flops 18874368 | bytes 31506944 | tf_op jit(solution)/shard_map/while/body/eval_jaxpr/convert_element_type | solution.py:239
  281.6 7.3 %multiply_reduce_fusion.10 = (f32[12,512]{1,0:T(8,128)S(1)}, f32[12,512,512]{1,2,0:T(8,128)}) fusion(f32[12,512,512]{1,2,0:T(8,128)S(1)} %fusion.139, f32[12,512]{1,0:T(8,128)S(1)} %dynamic-slice_bitcast_fusion.2, pred[512]{0:T(512)(128)(4,1)S(1)} %dynamic-slice_reduce_fusion.5, bf16[2,512,12,64]{1,3,2,0:T(8,128)(2,1)S(1)} %copy-done.3, ...), kind=kOutput, calls=%fused_computation.23.clone.1 | convolution fusion | flops 418375680 | bytes 26796552 | tf_op jit(solution)/shard_map/while/body/eval_jaxpr/qhd,khd->hqk/dot_general | solution.py:229
  288.9 7.2 %multiply_convert_fusion.2 = bf16[12,512,512]{1,2,0:T(8,128)(2,1)S(1)} fusion(f32[12,512,512]{1,2,0:T(8,128)} %get-tuple-element.599, f32[12,512,512]{1,2,0:T(8,128)S(1)} %fusion.139, f32[12,512]{1,0:T(8,128)S(1)} %get-tuple-element.600, f32[12,512]{1,0:T(8,128)S(1)} %dynamic-slice_bitcast_fusion.2, pred[512]{0:T(512)(128)(4,1)S(1)} %dynamic-slice_reduce_fusion.5), kind=kLoop, calls=%fused_computation.22.clone.1 | loop fusion | flops 18874368 | bytes 31506944 | tf_op jit(solution)/shard_map/while/body/eval_jaxpr/convert_element_type | solution.py:239
  327.1 9.9 %convolution_convert_fusion = bf16[3072,768]{1,0:T(8,128)(2,1)} fusion(bf16[1024,3072]{1,0:T(8,128)(2,1)} %get-tuple-element.468, f32[1024,768]{1,0:T(8,128)} %copy-done.19), kind=kOutput, calls=%fused_computation.82 | convolution fusion | flops 4834983936 | bytes 14155776 | tf_op jit(solution)/shard_map/rd,re->de/dot_general | solution.py:23
  338.9 10.0 %convolution_convert_fusion.1 = bf16[768,3072]{1,0:T(8,128)(2,1)} fusion(bf16[1024,3072]{1,0:T(8,128)(2,1)} %copy-done.63, f32[1024,768]{1,0:T(8,128)S(1)} %copy-done.8, f32[768]{0:T(1024)S(1)} %copy-done.50, f32[768]{0:T(1024)S(1)} %copy-done.40, f32[1024]{0:T(1024)S(1)} %copy-done.42, f32[1024]{0:T(1024)S(1)} %copy-done.37), kind=kOutput, calls=%fused_computation.83 | convolution fusion | flops 4838129664 | bytes 14170112 | tf_op jit(solution)/shard_map/rd,re->de/dot_general | solution.py:23
  354.6 23.1 %all-reduce.17 = (bf16[768]{0:T(1024)(128)(2,1)S(1)}, bf16[768]{0:T(1024)(128)(2,1)S(1)}, bf16[768]{0:T(1024)(128)(2,1)S(1)}, bf16[768]{0:T(1024)(128)(2,1)S(1)}...) all-reduce(bf16[768]{0:T(1024)(128)(2,1)S(1)} %dynamic-update-slice, ...), channel_id=1, replica_groups=mesh['group'=8,'replica'=4] {'group'}, use_global_device_ids=true, to_apply=%add.7 | all-reduce | flops 9984 | bytes 39936
  378.4 11.8 %all-reduce.19 = (bf16[96]{0:T(256)(128)(2,1)S(1)}, bf16[96]{0:T(256)(128)(2,1)S(1)}, bf16[96]{0:T(256)(128)(2,1)S(1)}, bf16[384]{0:T(512)(128)(2,1)S(1)}, bf16[...) all-reduce(bf16[96]{0:T(256)(128)(2,1)S(1)} %dynamic-slice.9, ...), channel_id=1, replica_groups=mesh['group'=8,'replica'=4] {'replica'}, use_global_device_ids=true, to_apply=%region_29.30 | all-reduce | flops 1152 | bytes 4608 | tf_op jit(solution)/shard_map/psum | solution.py:325
  398.3 27.5 %reduce-scatter.21.cloned.1.call-done = bf16[96,768]{1,0:T(8,128)(2,1)} async-done(((bf16[768,768]{1,0:T(8,128)(2,1)}), bf16[96,768]{1,0:T(8,128)(2,1)}) %reduce-scatter.21.cloned.1.call-update) | async-done | bytes 147472
  427.5 38.6 %reduce-scatter.13.cloned.1.call-done = bf16[96,768]{1,0:T(8,128)(2,1)} async-done(((bf16[768,768]{1,0:T(8,128)(2,1)}), bf16[96,768]{1,0:T(8,128)(2,1)}) %reduce-scatter.13.cloned.1.call-update) | async-done | bytes 147472 | tf_op jit(solution)/shard_map/reduce_scatter | solution.py:286
  466.2 57.3 %reduce-scatter.17.cloned.1.call-done = bf16[384,768]{1,0:T(8,128)(2,1)} async-done(((bf16[3072,768]{1,0:T(8,128)(2,1)}), bf16[384,768]{1,0:T(8,128)(2,1)}) %reduce-scatter.17.cloned.1.call-update) | async-done | bytes 589840 | tf_op jit(solution)/shard_map/reduce_scatter | solution.py:292
  523.4 57.1 %reduce-scatter.15.cloned.1.call-done = bf16[96,3072]{1,0:T(8,128)(2,1)} async-done(((bf16[768,3072]{1,0:T(8,128)(2,1)}), bf16[96,3072]{1,0:T(8,128)(2,1)}) %reduce-scatter.15.cloned.1.call-update) | async-done | bytes 589840 | tf_op jit(solution)/shard_map/reduce_scatter | solution.py:289
  590.1 74.7 %all-reduce.23.cloned.1.call-done = (bf16[96,768]{0,1:T(8,128)(2,1)}, bf16[96,768]{0,1:T(8,128)(2,1)}, bf16[96,768]{0,1:T(8,128)(2,1)}, bf16[96,768]{1,0:T(8,128...) async-done(((bf16[96,768]{0,1:T(8,128)(2,1)}, bf16[96,768]{0,1:T(8,128)(2,1)}, bf16[96,768]{0,1:T(8,128)(2,1)}, bf16[96,768]{1,0:T(8,128)(2,1)}, ...) | async-done | bytes 1769488 | tf_op jit(solution)/shard_map/psum | solution.py:325
  (325 shorter events, 174.2 us)
Async XLA Ops:
  7.2 51.7 %all-gather.8.cloned.1.call-start = ((), (), s32[]{:S(2)}) async-start(), calls=%async_computation.6 | async-start | bytes 1327104 | tf_op jit(solution)/shard_map/all_gather | solution.py:76
  7.9 57.6 %all-gather.10.cloned.1.call-start = ((), (), s32[]{:S(2)}) async-start(), calls=%async_computation.7 | async-start | bytes 1327104 | tf_op jit(solution)/shard_map/all_gather | solution.py:74
  8.7 79.7 %all-gather.12.cloned.1.call-start = ((), (), s32[]{:S(2)}) async-start(), calls=%async_computation.8 | async-start | bytes 1327104 | tf_op jit(solution)/shard_map/all_gather | solution.py:75
  9.4 119.2 %all-gather.14.cloned.1.call-start = ((), (), s32[]{:S(2)}) async-start(), calls=%async_computation.9 | async-start | bytes 1327104 | tf_op jit(solution)/shard_map/all_gather | solution.py:77
  10.0 144.6 %all-gather.16.cloned.1.call-start = ((), (), s32[]{:S(2)}) async-start(), calls=%async_computation.10 | async-start | bytes 5308416 | tf_op jit(solution)/shard_map/all_gather | solution.py:78
  10.6 184.6 %all-gather.18.cloned.1.call-start = ((), (), s32[]{:S(2)}) async-start(), calls=%async_computation.11 | async-start | bytes 5308416 | tf_op jit(solution)/shard_map/all_gather | solution.py:79
  11.1 383.7 %reduce-scatter.19.cloned.1.call-start = ((), (), s32[]{:S(2)}) async-start(), calls=%async_computation.15 | async-start | bytes 1327104
  45.7 185.7 %copy-start.39 = (f32[768]{0:T(1024)}, f32[768]{0:T(1024)S(1)}, u32[]{:S(2)}) copy-start(f32[768]{0:T(1024)S(1)} %convert_element_type.279) | copy-start | bytes 9220
  45.7 149.5 %copy-start.49 = (f32[768]{0:T(1024)}, f32[768]{0:T(1024)S(1)}, u32[]{:S(2)}) copy-start(f32[768]{0:T(1024)S(1)} %convert_element_type.280) | copy-start | bytes 9220
  132.6 98.8 %copy-start.36 = (f32[1024]{0:T(1024)}, f32[1024]{0:T(1024)S(1)}, u32[]{:S(2)}) copy-start(f32[1024]{0:T(1024)S(1)} %broadcast_multiply_fusion.4) | copy-start | bytes 12292
  134.7 96.7 %copy-start.41 = (f32[1024]{0:T(1024)}, f32[1024]{0:T(1024)S(1)}, u32[]{:S(2)}) copy-start(f32[1024]{0:T(1024)S(1)} %add_rsqrt_fusion.1) | copy-start | bytes 12292
  154.6 40.6 %copy-start.51 = (f32[768]{0:T(1024)S(1)}, f32[768]{0:T(1024)}, u32[]{:S(2)}) copy-start(f32[768]{0:T(1024)} %convert_element_type.284) | copy-start | bytes 9220
  209.2 15.6 %slice-start = ((s8[4718592]{0:T(1024)(128)(4,1)}), s8[4194304]{0:T(1024)(128)(4,1)S(1)}, s32[]{:S(2)}) async-start(s8[4718592]{0:T(1024)(128)(4,1)} %bitcast.210), calls=%async_computation.19 | async-start | bytes 8388608
  211.3 13.5 %slice-start.1 = ((s8[4718592]{0:T(1024)(128)(4,1)}), s8[524288]{0:T(1024)(128)(4,1)S(1)}, s32[]{:S(2)}) async-start(s8[4718592]{0:T(1024)(128)(4,1)} %bitcast.210), calls=%async_computation.20 | async-start | bytes 1048576
  308.4 88.2 %reduce-scatter.23.cloned.1.call-start = ((), (), s32[]{:S(2)}) async-start(), calls=%async_computation.17 | async-start | bytes 1327104
  314.8 111.0 %reduce-scatter.21.cloned.1.call-start = ((), (), s32[]{:S(2)}) async-start(), calls=%async_computation.16 | async-start | bytes 1327104
  323.1 143.0 %reduce-scatter.13.cloned.1.call-start = ((), (), s32[]{:S(2)}) async-start(), calls=%async_computation.12 | async-start | bytes 1327104 | tf_op jit(solution)/shard_map/reduce_scatter | solution.py:286
  327.0 196.4 %reduce-scatter.17.cloned.1.call-start = ((), (), s32[]{:S(2)}) async-start(), calls=%async_computation.14 | async-start | bytes 5308416 | tf_op jit(solution)/shard_map/reduce_scatter | solution.py:292
  337.0 243.5 %reduce-scatter.15.cloned.1.call-start = ((), (), s32[]{:S(2)}) async-start(), calls=%async_computation.13 | async-start | bytes 5308416 | tf_op jit(solution)/shard_map/reduce_scatter | solution.py:289
  349.0 231.6 %copy-start.1 = (f32[1024,768]{1,0:T(8,128)S(1)}, f32[1024,768]{1,0:T(8,128)}, u32[]{:S(2)}) copy-start(f32[1024,768]{1,0:T(8,128)} %copy-done) | copy-start | bytes 9437188
  349.0 231.6 %copy-start.31 = (f32[768]{0:T(1024)S(1)}, f32[768]{0:T(1024)}, u32[]{:S(2)}) copy-start(f32[768]{0:T(1024)} %copy-done.29) | copy-start | bytes 9220
  349.0 231.6 %copy-start.33 = (f32[1024]{0:T(1024)S(1)}, f32[1024]{0:T(1024)}, u32[]{:S(2)}) copy-start(f32[1024]{0:T(1024)} %copy-done.32) | copy-start | bytes 12292
  349.0 231.6 %copy-start.35 = (f32[1024]{0:T(1024)S(1)}, f32[1024]{0:T(1024)}, u32[]{:S(2)}) copy-start(f32[1024]{0:T(1024)} %copy-done.34) | copy-start | bytes 12292
  349.0 315.8 %all-reduce.23.cloned.1.call-start = ((), (), s32[]{:S(2)}) async-start(), calls=%async_computation.18 | async-start | bytes 3833856 | tf_op jit(solution)/shard_map/psum | solution.py:325
  (64 other events, 226.8 us)
Sparse Core Ops, SparseCore 0:
  9.9 26.7 all-gather.7
  38.5 23.9 all-gather.9
  64.4 23.9 all-gather.11
  90.1 23.9 all-gather.13
  115.8 38.7 all-gather.15
  156.3 38.7 all-gather.17
  308.5 36.6 reduce-scatter.18
  348.4 36.8 reduce-scatter.22
  389.1 36.6 reduce-scatter.20
  429.4 36.6 reduce-scatter.12
  469.6 53.7 reduce-scatter.16
  526.7 53.7 reduce-scatter.14
  583.9 80.8 all-reduce.22
where the time goes:
time: 690 us; the launch traced here: 682 us
  waiting for transfers between devices  300 us (43%)
  matrix products  163 us (24%)
  local copies, waits for them, and re-layouts  77.7 us (11%)
  blocking collectives  68.7 us (10%)
  other arithmetic  45.5 us (7%)
  between operations  17.2 us (2%)
  loops' own time  8.97 us (1%)
    psum x1, waiting for transfers between devices, per_device(): lax.psum(for_sending(tuple(owned)), 'replica')  74.7 us
    dot_general x6, matrix products, project(): return jnp.dot(left, right, preferred_element_type=jnp.float32)  60.8 us
    reduce_scatter x1, waiting for transfers between devices, per_device(): lax.psum_scatter(back_weight_grad.astype(jnp.bfloat16), 'group', scatter_...  57.3 us
    reduce_scatter x1, waiting for transfers between devices, per_device(): lax.psum_scatter(in_weight_grad.astype(jnp.bfloat16), 'group', scatter_di...  57.1 us
    unnamed x2, blocking collectives  49 us
    unnamed x156, local copies, waits for them, and re-layouts  41.7 us
    reduce_scatter x1, waiting for transfers between devices, per_device(): lax.psum_scatter(out_weight_grad.astype(jnp.bfloat16), 'group', scatter_d...  38.6 us
    unnamed x16, waiting for transfers between devices  31.2 us
  transfers between devices with their start and end apart: 13, of which 8 were waited for; matrix products, arithmetic and copies ran while one was open for 23% of the time, Pallas kernels for 0%

commit v1 on v0

--- a/solution.py
+++ b/solution.py
@@ -9,6 +9,28 @@
 NORM_EPS = 1e-12
 inverse_root_two = 0.7071067811865476
 inverse_root_tau = 0.3989422804014327
+
+
+def in_order(blocks, dim):
+    blocks = jnp.moveaxis(blocks, 0, dim)
+    lengths = blocks.shape
+    return blocks.reshape(*lengths[:dim], lengths[dim] * lengths[dim + 1], *lengths[dim + 2 :])
+
+
+def doubled(shard, axis):
+    count = lax.axis_size(axis)
+    blocks = shard[None]
+    for level in range(count.bit_length() - 1):
+        distance = 1 << level
+        other = lax.ppermute(blocks, axis, [(i, i ^ distance) for i in range(count)])
+        both = jnp.stack([blocks, other])
+        upper = lax.axis_index(axis) >> level & 1
+        blocks = jnp.where(upper == 0, both, both[::-1]).reshape(-1, *shard.shape)
+    return blocks
+
+
+def collect(shard, axis, dim):
+    return in_order(doubled(shard, axis), dim)
 
 
 def for_sending(array):
@@ -72,7 +94,7 @@
 ):
     whole = (
         lax.all_gather(query_weight, "group", axis=0, tiled=True),
-        lax.all_gather(key_weight, "group", axis=0, tiled=True),
+        collect(key_weight, "group", 0),
         lax.all_gather(value_weight, "group", axis=0, tiled=True),
         lax.all_gather(out_weight, "group", axis=0, tiled=True),
         lax.all_gather(in_weight, "group", axis=0, tiled=True),

time: 690 us -> 694 us (level)
  blocking collectives: 68.7 us -> 75.7 us
  waiting for transfers between devices: 300 us -> 293 us
    all_gather x1, waiting for transfers between devices: 19.9 us -> 7.26 us  [per_device(): lax.all_gather(in_weight, 'group', axis=0, tiled=True)]
    all_gather x1, blocking collectives: 7.91 us -> 15.4 us  [per_device(): lax.all_gather(in_bias, 'group', axis=0, tiled=True)]
    unnamed x156 -> x178, local copies, waits for them, and re-layouts: 41.7 us -> 34.5 us
  transfers between devices with their start and end apart: 13 -> 16, of which waited for: 8 -> 9; matrix products, arithmetic and copies ran while one was open for 23% -> 23% of each run, Pallas kernels for 0% -> 0%
where the time goes in v1:
time: 694 us; the launch traced here: 685 us
  waiting for transfers between devices  293 us (42%)
  matrix products  166 us (24%)
  blocking collectives  75.7 us (11%)
  local copies, waits for them, and re-layouts  73.3 us (11%)
  other arithmetic  44.8 us (6%)
  between operations  17.4 us (3%)
  loops' own time  8.97 us (1%)
    psum x1, waiting for transfers between devices, per_device(): lax.psum(for_sending(tuple(owned)), 'replica')  77.9 us
    dot_general x6, matrix products, project(): return jnp.dot(left, right, preferred_element_type=jnp.float32)  60.2 us
    reduce_scatter x1, waiting for transfers between devices, per_device(): lax.psum_scatter(in_weight_grad.astype(jnp.bfloat16), 'group', scatter_di...  57.2 us
    reduce_scatter x1, waiting for transfers between devices, per_device(): lax.psum_scatter(back_weight_grad.astype(jnp.bfloat16), 'group', scatter_...  57.1 us
    unnamed x2, blocking collectives  48.4 us
    reduce_scatter x1, waiting for transfers between devices, per_device(): lax.psum_scatter(out_weight_grad.astype(jnp.bfloat16), 'group', scatter_d...  38.8 us
    unnamed x178, local copies, waits for them, and re-layouts  34.5 us
    dot_general x6, matrix products, back_project(): jnp.einsum('re,de->rd', grad_rows, weight_full, preferred_element_type=jn...  31.9 us
  transfers between devices with their start and end apart: 16, of which 9 were waited for; matrix products, arithmetic and copies ran while one was open for 23% of the time, Pallas kernels for 0%

profile of v1, /device:TPU:0, one launch (start us, length us, event | category | flops | bytes accessed | tf_op | source)
XLA Modules:
  0.0 685.1 jit_solution(6678811101032192082)
XLA Ops:
  18.9 25.1 %all-reduce.18 = (bf16[768]{0:T(1024)(128)(2,1)S(1)}, bf16[768]{0:T(1024)(128)(2,1)S(1)}, bf16[768]{0:T(1024)(128)(2,1)S(1)}, bf16[768]{0:T(1024)(128)(2,1)S(1)}...) all-reduce(bf16[768]{0:T(1024)(128)(2,1)S(1)} %dynamic-update-slice, ...), channel_id=1, replica_groups=mesh['group'=8,'replica'=4] {'group'}, use_global_device_ids=true, to_apply=%add.1 | all-reduce | flops 5376 | bytes 21504
  49.0 15.4 %all-gather = bf16[8,1,384]{2,1,0:T(2,128)(2,1)S(1)} all-gather(bf16[1,1,384]{2,1,0:T(2,128)(2,1)S(1)} %reshape.256), channel_id=1, replica_groups=mesh['group'=8,'replica'=4] {'group'}, dimensions={0}, use_global_device_ids=true | all-gather | bytes 6912 | tf_op jit(solution)/shard_map/all_gather | solution.py:105
  67.8 4.3 add_convert_fusion.3
  88.7 25.4 %while.30 = (s32[]{:T(128)}, bf16[2,512,12,64]{1,3,2,0:T(8,128)(2,1)}, f32[2,12,512]{2,1,0:T(8,128)S(1)}, s32[2]{0:T(128)S(1)}, bf16[2,512,12,64]{1,3,2,0:T(8,12...) while((s32[]{:T(128)}, ...), condition=%wide.region_3.4_spmd, body=%wide.region_0.3_spmd.sunk | while | flops 843442176 | bytes 47426260 | solution.py:177
  124.9 7.3 %all-gather.14.cloned.1.call-done = bf16[768,3072]{1,0:T(8,128)(2,1)} async-done(((bf16[96,3072]{1,0:T(8,128)(2,1)}), bf16[768,3072]{1,0:T(8,128)(2,1)}) %all-gather.14.cloned.1.call-update) | async-done | bytes 4718608 | tf_op jit(solution)/shard_map/all_gather | solution.py:100
  132.1 37.4 %fusion.48 = (bf16[1024,3072]{1,0:T(8,128)(2,1)}, f32[1024,3072]{1,0:T(8,128)}) fusion(f32[3072]{0:T(1024)S(1)} %bitcast.230, bf16[768,3072]{1,0:T(8,128)(2,1)} %all-gather.14.cloned.1.call-done, f32[1024,768]{1,0:T(8,128)} %copy-done.7, f32[768]{0:T(1024)S(1)} %convert_element_type.284, f32[768]{0:T(1024)S(1)} %convert_element_type.283, ...), kind=kOutput, calls=%fused_computation.60 | convolution fusion | flops 5043388416 | bytes 26765312 | tf_op jit(solution)/shard_map/dot_general | solution.py:41
  172.7 9.3 %fusion.81 = (f32[1024]{0:T(1024)S(1)}, f32[1024,768]{1,0:T(8,128)S(1)}) fusion(f32[768]{0:T(1024)S(1)} %copy-done.52, bf16[1024,3072]{1,0:T(8,128)(2,1)} %get-tuple-element.470, bf16[3072,768]{1,0:T(8,128)(2,1)} %all-gather.16.cloned.1.call-done, f32[768]{0:T(1024)S(1)} %convert_element_type.284, f32[768]{0:T(1024)S(1)} %convert_element_type.283, ...), kind=kOutput, calls=%fused_computation.147 | convolution fusion | flops 4837342208 | bytes 17323008 | tf_op jit(solution)/shard_map/dot_general | solution.py:41
  188.9 13.5 %fusion.82 = (bf16[3072]{0:T(1024)(128)(2,1)}, bf16[1024,3072]{1,0:T(8,128)(2,1)S(1)}) fusion(f32[1024,3072]{1,0:T(8,128)} %get-tuple-element.471, f32[3072]{0:T(1024)S(1)} %bitcast.231, bf16[3072,768]{1,0:T(8,128)(2,1)S(1)} %copy-done.58, f32[1024,768]{1,0:T(8,128)S(1)} %get-tuple-element.454), kind=kOutput, calls=%fused_computation.148 | convolution fusion | flops 4870370304 | bytes 26757120 | tf_op jit(solution)/shard_map/re,de->rd/dot_general | solution.py:49
  202.3 6.6 multiply_reduce_fusion.2
  224.3 53.9 %while.31 = (s32[]{:T(128)}, bf16[2,512,12,64]{1,3,2,0:T(8,128)(2,1)}, bf16[2,512,12,64]{1,3,2,0:T(8,128)(2,1)}, bf16[2,512,12,64]{1,3,2,0:T(8,128)(2,1)}, s32[2...) while((s32[]{:T(128)}, ...), condition=%wide.region_14.15_spmd, body=%wide.region_12.14_spmd.sunk | while | flops 2061232128 | bytes 155120608 | solution.py:272
  232.3 7.3 %multiply_reduce_fusion.10 = (f32[12,512]{1,0:T(8,128)S(1)}, f32[12,512,512]{1,2,0:T(8,128)}) fusion(f32[12,512,512]{1,2,0:T(8,128)S(1)} %fusion.142, f32[12,512]{1,0:T(8,128)S(1)} %dynamic-slice_bitcast_fusion.2, pred[512]{0:T(512)(128)(4,1)S(1)} %dynamic-slice_reduce_fusion.5, bf16[2,512,12,64]{1,3,2,0:T(8,128)(2,1)S(1)} %copy-done.3, ...), kind=kOutput, calls=%fused_computation.23.clone.1 | convolution fusion | flops 418375680 | bytes 26796552 | tf_op jit(solution)/shard_map/while/body/eval_jaxpr/qhd,khd->hqk/dot_general | solution.py:251
  239.6 7.2 %multiply_convert_fusion.2 = bf16[12,512,512]{1,2,0:T(8,128)(2,1)S(1)} fusion(f32[12,512,512]{1,2,0:T(8,128)} %get-tuple-element.601, f32[12,512,512]{1,2,0:T(8,128)S(1)} %fusion.142, f32[12,512]{1,0:T(8,128)S(1)} %get-tuple-element.602, f32[12,512]{1,0:T(8,128)S(1)} %dynamic-slice_bitcast_fusion.2, pred[512]{0:T(512)(128)(4,1)S(1)} %dynamic-slice_reduce_fusion.5), kind=kLoop, calls=%fused_computation.22.clone.1 | loop fusion | flops 18874368 | bytes 31506944 | tf_op jit(solution)/shard_map/while/body/eval_jaxpr/convert_element_type | solution.py:261
  259.0 7.3 %multiply_reduce_fusion.10 = (f32[12,512]{1,0:T(8,128)S(1)}, f32[12,512,512]{1,2,0:T(8,128)}) fusion(f32[12,512,512]{1,2,0:T(8,128)S(1)} %fusion.142, f32[12,512]{1,0:T(8,128)S(1)} %dynamic-slice_bitcast_fusion.2, pred[512]{0:T(512)(128)(4,1)S(1)} %dynamic-slice_reduce_fusion.5, bf16[2,512,12,64]{1,3,2,0:T(8,128)(2,1)S(1)} %copy-done.3, ...), kind=kOutput, calls=%fused_computation.23.clone.1 | convolution fusion | flops 418375680 | bytes 26796552 | tf_op jit(solution)/shard_map/while/body/eval_jaxpr/qhd,khd->hqk/dot_general | solution.py:251
  266.3 7.2 %multiply_convert_fusion.2 = bf16[12,512,512]{1,2,0:T(8,128)(2,1)S(1)} fusion(f32[12,512,512]{1,2,0:T(8,128)} %get-tuple-element.601, f32[12,512,512]{1,2,0:T(8,128)S(1)} %fusion.142, f32[12,512]{1,0:T(8,128)S(1)} %get-tuple-element.602, f32[12,512]{1,0:T(8,128)S(1)} %dynamic-slice_bitcast_fusion.2, pred[512]{0:T(512)(128)(4,1)S(1)} %dynamic-slice_reduce_fusion.5), kind=kLoop, calls=%fused_computation.22.clone.1 | loop fusion | flops 18874368 | bytes 31506944 | tf_op jit(solution)/shard_map/while/body/eval_jaxpr/convert_element_type | solution.py:261
  304.6 9.9 %convolution_convert_fusion = bf16[3072,768]{1,0:T(8,128)(2,1)} fusion(bf16[1024,3072]{1,0:T(8,128)(2,1)} %get-tuple-element.470, f32[1024,768]{1,0:T(8,128)} %copy-done.20), kind=kOutput, calls=%fused_computation.82 | convolution fusion | flops 4834983936 | bytes 14155776 | tf_op jit(solution)/shard_map/rd,re->de/dot_general | solution.py:45
  316.3 10.0 %convolution_convert_fusion.1 = bf16[768,3072]{1,0:T(8,128)(2,1)} fusion(bf16[1024,3072]{1,0:T(8,128)(2,1)} %copy-done.74, f32[1024,768]{1,0:T(8,128)S(1)} %copy-done.9, f32[768]{0:T(1024)S(1)} %copy-done.51, f32[768]{0:T(1024)S(1)} %copy-done.41, f32[1024]{0:T(1024)S(1)} %copy-done.43, f32[1024]{0:T(1024)S(1)} %copy-done.38), kind=kOutput, calls=%fused_computation.83 | convolution fusion | flops 4838129664 | bytes 14170112 | tf_op jit(solution)/shard_map/rd,re->de/dot_general | solution.py:45
  332.6 23.3 %all-reduce.17 = (bf16[768]{0:T(1024)(128)(2,1)S(1)}, bf16[768]{0:T(1024)(128)(2,1)S(1)}, bf16[768]{0:T(1024)(128)(2,1)S(1)}, bf16[768]{0:T(1024)(128)(2,1)S(1)}...) all-reduce(bf16[768]{0:T(1024)(128)(2,1)S(1)} %dynamic-update-slice, ...), channel_id=1, replica_groups=mesh['group'=8,'replica'=4] {'group'}, use_global_device_ids=true, to_apply=%add.7 | all-reduce | flops 9984 | bytes 39936
  356.5 11.8 %all-reduce.19 = (bf16[96]{0:T(256)(128)(2,1)S(1)}, bf16[96]{0:T(256)(128)(2,1)S(1)}, bf16[96]{0:T(256)(128)(2,1)S(1)}, bf16[384]{0:T(512)(128)(2,1)S(1)}, bf16[...) all-reduce(bf16[96]{0:T(256)(128)(2,1)S(1)} %dynamic-slice.9, ...), channel_id=1, replica_groups=mesh['group'=8,'replica'=4] {'replica'}, use_global_device_ids=true, to_apply=%region_29.30 | all-reduce | flops 1152 | bytes 4608 | tf_op jit(solution)/shard_map/psum | solution.py:347
  376.5 26.7 %reduce-scatter.21.cloned.1.call-done = bf16[96,768]{1,0:T(8,128)(2,1)} async-done(((bf16[768,768]{1,0:T(8,128)(2,1)}), bf16[96,768]{1,0:T(8,128)(2,1)}) %reduce-scatter.21.cloned.1.call-update) | async-done | bytes 147472
  405.0 38.8 %reduce-scatter.13.cloned.1.call-done = bf16[96,768]{1,0:T(8,128)(2,1)} async-done(((bf16[768,768]{1,0:T(8,128)(2,1)}), bf16[96,768]{1,0:T(8,128)(2,1)}) %reduce-scatter.13.cloned.1.call-update) | async-done | bytes 147472 | tf_op jit(solution)/shard_map/reduce_scatter | solution.py:308
  443.7 57.1 %reduce-scatter.17.cloned.1.call-done = bf16[384,768]{1,0:T(8,128)(2,1)} async-done(((bf16[3072,768]{1,0:T(8,128)(2,1)}), bf16[384,768]{1,0:T(8,128)(2,1)}) %reduce-scatter.17.cloned.1.call-update) | async-done | bytes 589840 | tf_op jit(solution)/shard_map/reduce_scatter | solution.py:314
  500.8 57.2 %reduce-scatter.15.cloned.1.call-done = bf16[96,3072]{1,0:T(8,128)(2,1)} async-done(((bf16[768,3072]{1,0:T(8,128)(2,1)}), bf16[96,3072]{1,0:T(8,128)(2,1)}) %reduce-scatter.15.cloned.1.call-update) | async-done | bytes 589840 | tf_op jit(solution)/shard_map/reduce_scatter | solution.py:311
  563.5 20.2 %all-gather.18.cloned.1.call-done = bf16[768,768]{1,0:T(8,128)(2,1)} async-done(((bf16[96,768]{1,0:T(8,128)(2,1)}), bf16[768,768]{1,0:T(8,128)(2,1)}) %all-gather.18.cloned.1.call-update) | async-done | bytes 1179664 | tf_op jit(solution)/shard_map/all_gather | solution.py:195
  590.2 77.9 %all-reduce.23.cloned.1.call-done = (bf16[96,768]{0,1:T(8,128)(2,1)}, bf16[96,768]{0,1:T(8,128)(2,1)}, bf16[96,768]{0,1:T(8,128)(2,1)}, bf16[96,768]{1,0:T(8,128...) async-done(((bf16[96,768]{0,1:T(8,128)(2,1)}, bf16[96,768]{0,1:T(8,128)(2,1)}, bf16[96,768]{0,1:T(8,128)(2,1)}, bf16[96,768]{1,0:T(8,128)(2,1)}, ...) | async-done | bytes 1769488 | tf_op jit(solution)/shard_map/psum | solution.py:347
  (358 shorter events, 177.8 us)
Async XLA Ops:
  7.3 60.4 %all-gather.8.cloned.1.call-start = ((), (), s32[]{:S(2)}) async-start(), calls=%async_computation.6 | async-start | bytes 1327104 | tf_op jit(solution)/shard_map/all_gather | solution.py:98
  8.0 71.1 %all-gather.10.cloned.1.call-start = ((), (), s32[]{:S(2)}) async-start(), calls=%async_computation.7 | async-start | bytes 1327104 | tf_op jit(solution)/shard_map/all_gather | solution.py:96
  8.8 110.0 %all-gather.12.cloned.1.call-start = ((), (), s32[]{:S(2)}) async-start(), calls=%async_computation.8 | async-start | bytes 1327104 | tf_op jit(solution)/shard_map/all_gather | solution.py:99
  9.5 122.6 %all-gather.14.cloned.1.call-start = ((), (), s32[]{:S(2)}) async-start(), calls=%async_computation.9 | async-start | bytes 5308416 | tf_op jit(solution)/shard_map/all_gather | solution.py:100
  10.1 162.6 %all-gather.16.cloned.1.call-start = ((), (), s32[]{:S(2)}) async-start(), calls=%async_computation.10 | async-start | bytes 5308416 | tf_op jit(solution)/shard_map/all_gather | solution.py:101
  10.1 1.8 collective-permute-start
  12.9 31.8 %collective-permute-start.1 = (bf16[2,96,768]{2,1,0:T(8,128)(2,1)S(1)}, bf16[2,96,768]{2,1,0:T(8,128)(2,1)S(1)}, u32[]{:S(2)}, u32[]{:S(2)}) collective-permute-start(bf16[2,96,768]{2,1,0:T(8,128)(2,1)S(1)} %get-tuple-element.462), channel_id=1, source_target_pairs={{0,8},{4,12},{8,0},{12,4},{16,24},{20,28},{24,16},{28,20},{1,9},{5... | collective-permute-start | bytes 884744 | tf_op jit(solution)/shard_map/ppermute | solution.py:25
  15.9 357.2 %reduce-scatter.19.cloned.1.call-start = ((), (), s32[]{:S(2)}) async-start(), calls=%async_computation.15 | async-start | bytes 1327104
  44.1 164.8 %copy-start.40 = (f32[768]{0:T(1024)}, f32[768]{0:T(1024)S(1)}, u32[]{:S(2)}) copy-start(f32[768]{0:T(1024)S(1)} %convert_element_type.283) | copy-start | bytes 9220
  44.1 128.6 %copy-start.50 = (f32[768]{0:T(1024)}, f32[768]{0:T(1024)S(1)}, u32[]{:S(2)}) copy-start(f32[768]{0:T(1024)S(1)} %convert_element_type.284) | copy-start | bytes 9220
  44.9 19.5 %collective-permute-start.2 = (bf16[4,96,768]{2,1,0:T(8,128)(2,1)S(1)}, bf16[4,96,768]{2,1,0:T(8,128)(2,1)S(1)}, u32[]{:S(2)}, u32[]{:S(2)}) collective-permute-start(bf16[4,96,768]{2,1,0:T(8,128)(2,1)S(1)} %bitcast.211), channel_id=1, source_target_pairs={{0,16},{4,20},{8,24},{12,28},{16,0},{20,4},{24,8},{28,12},{1,17},{... | collective-permute-start | bytes 1769480 | tf_op jit(solution)/shard_map/ppermute | solution.py:25
  122.7 86.2 %copy-start.37 = (f32[1024]{0:T(1024)}, f32[1024]{0:T(1024)S(1)}, u32[]{:S(2)}) copy-start(f32[1024]{0:T(1024)S(1)} %broadcast_multiply_fusion.4) | copy-start | bytes 12292
  124.8 84.1 %copy-start.42 = (f32[1024]{0:T(1024)}, f32[1024]{0:T(1024)S(1)}, u32[]{:S(2)}) copy-start(f32[1024]{0:T(1024)S(1)} %add_rsqrt_fusion.1) | copy-start | bytes 12292
  285.8 89.0 %reduce-scatter.23.cloned.1.call-start = ((), (), s32[]{:S(2)}) async-start(), calls=%async_computation.17 | async-start | bytes 1327104
  292.2 111.0 %reduce-scatter.21.cloned.1.call-start = ((), (), s32[]{:S(2)}) async-start(), calls=%async_computation.16 | async-start | bytes 1327104
  300.6 143.1 %reduce-scatter.13.cloned.1.call-start = ((), (), s32[]{:S(2)}) async-start(), calls=%async_computation.12 | async-start | bytes 1327104 | tf_op jit(solution)/shard_map/reduce_scatter | solution.py:308
  304.5 196.3 %reduce-scatter.17.cloned.1.call-start = ((), (), s32[]{:S(2)}) async-start(), calls=%async_computation.14 | async-start | bytes 5308416 | tf_op jit(solution)/shard_map/reduce_scatter | solution.py:314
  314.5 243.6 %reduce-scatter.15.cloned.1.call-start = ((), (), s32[]{:S(2)}) async-start(), calls=%async_computation.13 | async-start | bytes 5308416 | tf_op jit(solution)/shard_map/reduce_scatter | solution.py:311
  326.5 257.3 %all-gather.18.cloned.1.call-start = ((), (), s32[]{:S(2)}) async-start(), calls=%async_computation.11 | async-start | bytes 1327104 | tf_op jit(solution)/shard_map/all_gather | solution.py:195
  327.0 231.0 %copy-start.1 = (f32[1024,768]{1,0:T(8,128)S(1)}, f32[1024,768]{1,0:T(8,128)}, u32[]{:S(2)}) copy-start(f32[1024,768]{1,0:T(8,128)} %copy-done) | copy-start | bytes 9437188
  327.0 231.0 %copy-start.32 = (f32[768]{0:T(1024)S(1)}, f32[768]{0:T(1024)}, u32[]{:S(2)}) copy-start(f32[768]{0:T(1024)} %copy-done.30) | copy-start | bytes 9220
  327.1 231.0 %copy-start.34 = (f32[1024]{0:T(1024)S(1)}, f32[1024]{0:T(1024)}, u32[]{:S(2)}) copy-start(f32[1024]{0:T(1024)} %copy-done.33) | copy-start | bytes 12292
  327.1 231.0 %copy-start.36 = (f32[1024]{0:T(1024)S(1)}, f32[1024]{0:T(1024)}, u32[]{:S(2)}) copy-start(f32[1024]{0:T(1024)} %copy-done.35) | copy-start | bytes 12292
  327.1 340.9 %all-reduce.23.cloned.1.call-start = ((), (), s32[]{:S(2)}) async-start(), calls=%async_computation.18 | async-start | bytes 3833856 | tf_op jit(solution)/shard_map/psum | solution.py:347
  (78 other events, 534.2 us)
Sparse Core Ops, SparseCore 0:
  10.0 28.1 all-gather.7
  40.1 25.5 all-gather.9
  67.6 23.9 all-gather.11
  93.3 38.7 all-gather.13
  133.8 38.7 all-gather.15
  285.9 36.6 reduce-scatter.18
  325.9 36.8 reduce-scatter.22
  366.5 36.6 reduce-scatter.20
  407.0 36.6 reduce-scatter.12
  447.0 53.7 reduce-scatter.16
  504.3 53.7 reduce-scatter.14
  559.8 23.9 all-gather.17
  587.2 80.7 all-reduce.22
